TPU v7x, 256 devices: a whole 4x4x8 slice. The times are simulated.
256 devices in a mesh: section: 16 (over y_hi, z), mp: 16 (over y_lo, x, core).
Axes of the slice: x: 4, y: 4 (y_hi: 2, y_lo: 2; y = y_hi * 2 + y_lo), z: 8, core: 2. Of those that a mesh axis runs over, the one named last changes fastest.
Arguments:
- pixels: bfloat16 [2048, 12, 256], P('mp')
- band_pick: int32 [16, 4], replicated, may hold values from 0 to 11, as said below
- band_count: int32 [16], replicated, may hold values from 1 to 4, as said below
- tok_gain: float32 [16, 7168], P(None, 'mp'), may hold values from 0.1 to 1.9
- bands_weight: bfloat16 [12, 256, 7168], P(None, None, 'mp')
- plan: int32 [4], replicated, may hold values from 0 to 3, each once
- trunk_gain: float32 [7168], replicated, may hold values from 0.1 to 1.9
- query_weight: bfloat16 [7168, 7168], P(None, 'mp'), may hold values from -0.0625 to 0.0625
- query_cot: bfloat16 [2048, 7168], P('section', 'mp'), may hold values from -6 to 6
- resid_cot: bfloat16 [2048, 7168], P('section', 'mp'), may hold values from -1.5 to 1.5
Outputs:
- queries: bfloat16 [2048, 7168], P('section', 'mp')
- band_grads: bfloat16 [12, 256, 7168], P(None, 'section', 'mp')
Inputs may be any that keep to these rules, and one draw needn't show every extreme that they name: Each row of band_pick names 4 different bands. Group g reads the first band_count[g] slots of its row; some group reads 4 bands and some group one.
All inputs are finite; a program needn't handle non-finite values.
Results may differ from a plain program's by a relative error of at most 0.0058.
Values may be sent and summed in bfloat16 or wider, within the bound.
A program may use at most 128 MiB of HBM per device.

v0:
```python
import jax
import jax.numpy as jnp
from jax import lax
from jax.sharding import PartitionSpec as P

EPSILON = 1e-05


def body(
    pixels,
    band_pick,
    band_count,
    tok_gain,
    bands_weight,
    plan,
    trunk_gain,
    query_weight,
    query_cot,
    resid_cot,
):
    mp_size = lax.axis_size("mp")
    section_index = lax.axis_index("section")
    slot_count = band_pick.shape[1]
    band_total = bands_weight.shape[0]
    patch_size = bands_weight.shape[1]
    cols_dev = bands_weight.shape[2]
    model_width = cols_dev * mp_size
    micro_count = plan.shape[0]
    picked = lax.dynamic_index_in_dim(band_pick, section_index, 0, keepdims=False)
    used_count = lax.dynamic_index_in_dim(band_count, section_index, 0, keepdims=False)
    gain_row = lax.dynamic_index_in_dim(tok_gain, section_index, 0, keepdims=False)
    live_slots = jnp.arange(slot_count) < used_count
    onehot = jnp.logical_and(
        picked[:, None] == jnp.arange(band_total)[None, :], live_slots[:, None]
    )
    onehot_low = onehot.astype(jnp.bfloat16)
    chosen = jnp.einsum(
        "tbp,kb->tkp", pixels, onehot_low, preferred_element_type=jnp.float32
    ).astype(jnp.bfloat16)
    gathered = lax.all_gather(chosen, "mp", axis=0, tiled=True)
    token_total = gathered.shape[0]
    flat_pixels = gathered.reshape(token_total, slot_count * patch_size)
    slot_weights = jnp.einsum(
        "kb,bpd->kpd", onehot_low, bands_weight, preferred_element_type=jnp.float32
    ).astype(jnp.bfloat16)
    flat_weights = slot_weights.reshape(slot_count * patch_size, cols_dev)
    group_out = jnp.dot(flat_pixels, flat_weights, preferred_element_type=jnp.float32)
    square_sums = lax.psum(jnp.sum(group_out * group_out, axis=1), "mp")
    group_scale = lax.rsqrt(square_sums / model_width + EPSILON)
    group_term = group_out * group_scale[:, None] * gain_row[None, :]
    micro_rows = token_total // micro_count
    reordered = jnp.take(
        group_term.reshape(micro_count, micro_rows, cols_dev), plan, axis=0
    ).reshape(token_total, cols_dev)
    trunk_sum = lax.psum_scatter(reordered, "section", scatter_dimension=0, tiled=True)
    trunk_in = trunk_sum.astype(jnp.bfloat16)
    full_rows = lax.all_gather(trunk_in, "mp", axis=1, tiled=True).astype(jnp.float32)
    row_scale = lax.rsqrt(jnp.mean(full_rows * full_rows, axis=1) + EPSILON)
    normed = (full_rows * row_scale[:, None] * trunk_gain[None, :]).astype(jnp.bfloat16)
    queries = jnp.dot(normed, query_weight, preferred_element_type=jnp.float32).astype(jnp.bfloat16)
    cross_terms = lax.dot_general(
        query_cot, query_weight, (((1,), (1,)), ((), ())), preferred_element_type=jnp.float32
    )
    col_start = lax.axis_index("mp") * cols_dev
    gain_cols = lax.dynamic_slice_in_dim(trunk_gain, col_start, cols_dev, 0)
    own_rows = trunk_in.astype(jnp.float32)
    grad_cols = lax.psum_scatter(cross_terms, "mp", scatter_dimension=1, tiled=True)
    row_stat = (
        lax.psum(jnp.sum(own_rows * gain_cols[None, :] * grad_cols, axis=1), "mp") / model_width
    )
    norm_grad = (
        row_scale[:, None] * gain_cols[None, :] * grad_cols
        - own_rows * (row_scale**3)[:, None] * row_stat[:, None]
    )
    input_grad = (resid_cot.astype(jnp.float32) + norm_grad).astype(jnp.bfloat16)
    all_grads = lax.all_gather(input_grad, "section", axis=0, tiled=True)
    inverse = jnp.sum(
        jnp.arange(micro_count)[:, None] * (plan[:, None] == jnp.arange(micro_count)[None, :]),
        axis=0,
    )
    embed_grad = jnp.take(
        all_grads.reshape(micro_count, micro_rows, cols_dev), inverse, axis=0
    ).reshape(token_total, cols_dev)
    unit_grad = embed_grad.astype(jnp.float32) * gain_row[None, :]
    group_stat = lax.psum(jnp.sum(group_out * unit_grad, axis=1), "mp") / model_width
    group_grad = (
        group_scale[:, None] * unit_grad
        - group_out * (group_scale**3)[:, None] * group_stat[:, None]
    ).astype(jnp.bfloat16)
    slot_grads = lax.dot_general(
        flat_pixels, group_grad, (((0,), (0,)), ((), ())), preferred_element_type=jnp.float32
    ).reshape(slot_count, patch_size, cols_dev)
    per_band = jnp.einsum(
        "kb,kpd->bpd", onehot.astype(jnp.float32), slot_grads, precision=lax.Precision.HIGHEST
    )
    band_grads = lax.psum_scatter(per_band, "section", scatter_dimension=1, tiled=True)
    return (queries, band_grads.astype(jnp.bfloat16))


def solution(mesh):
    placed = (
        P("mp", None, None),
        P(),
        P(),
        P(None, "mp"),
        P(None, None, "mp"),
        P(),
        P(),
        P(None, "mp"),
        P("section", "mp"),
        P("section", "mp"),
    )
    return jax.shard_map(
        body,
        mesh=mesh,
        in_specs=placed,
        out_specs=(P("section", "mp"), P(None, "section", "mp")),
        check_vma=False,
    )
```

profile of v0, /device:TPU:1, one launch (start us, length us, event | category | flops | bytes accessed | tf_op | source)
XLA Modules:
  0.0 741.3 jit_solution(13253204349163622760)
XLA Ops:
  7.2 0.0 copy-start
  7.2 0.0 all-gather.4.cloned.1.call-start
  7.2 1.4 dynamic_slice.16
  8.6 0.6 iota_compare_fusion.2
  9.3 0.9 dynamic-slice_reduce_fusion
  10.2 2.4 fusion.26
  12.5 0.0 all-gather.4.cloned.1.call-update
  12.6 0.0 reduce-scatter.6.cloned.1.call-start
  12.6 7.8 %fusion.48 = f32[128,7168]{0,1:T(8,128)} fusion(bf16[128,448]{0,1:T(8,128)(2,1)} %param.18, bf16[7168,448]{0,1:T(8,128)(2,1)} %param.17), kind=kOutput, calls=%fused_computation.76 | convolution fusion | flops 822083584 | bytes 10207232 | tf_op jit(solution)/shard_map/dot_general | solution.py:61
  20.4 0.0 copy-start.5
  20.4 0.0 reduce-scatter.6.cloned.1.call-update
  20.4 0.0 reduce-scatter.4.cloned.1.call-start
  20.5 0.6 copy-done.5
  21.0 0.1 select_reduce_fusion
  21.1 0.1 broadcast_bitcast_fusion.1
  21.2 0.7 constant_dynamic-slice_fusion
  22.0 0.0 copy-done
  22.0 2.7 fusion.23
  24.6 0.0 copy-start.3
  24.6 31.9 %all-gather.4.cloned.1.call-done = bf16[2048,4,256]{2,1,0:T(4,128)(2,1)} async-done(((bf16[128,4,256]{2,1,0:T(4,128)(2,1)}), bf16[2048,4,256]{2,1,0:T(4,128)(2,1)}) %all-gather.4.cloned.1.call-update) | async-done | bytes 4194320 | tf_op jit(solution)/shard_map/all_gather | solution.py:40
  56.5 7.6 %copy.48 = bf16[2048,4,256]{0,2,1:T(8,128)(2,1)} copy(bf16[2048,4,256]{2,1,0:T(4,128)(2,1)} %all-gather.4.cloned.1.call-done) | data formatting | bytes 8388608 | tf_op jit(solution)/shard_map/all_gather | solution.py:40
  64.1 0.0 copy-done.3
  64.1 6.1 fusion.5
  70.2 27.3 %psum.21 = f32[2048]{0:T(1024)S(1)} all-reduce(f32[2048]{0:T(1024)S(1)} %get-tuple-element.16), channel_id=1, replica_groups=mesh['section'=16,'mp'=16] {'mp'}, use_global_device_ids=true, to_apply=%region_1.2 | all-reduce | flops 2048 | bytes 16384 | tf_op jit(solution)/shard_map/psum | solution.py:48
  97.5 2.4 fusion.6
  99.9 2.3 copy.68
  102.2 4.6 gather_fusion
  106.8 2.5 copy.52
  109.3 2.3 broadcast_select_fusion
  111.6 0.0 copy-start.6
  111.6 0.0 reduce-scatter.4.cloned.1.call-update
  111.6 0.0 all-gather.6.cloned.1.call-start
  111.7 0.7 copy-done.6
  112.3 0.1 dynamic_slice.18
  112.4 12.2 %reduce-scatter.6.cloned.1.call-done = f32[128,448]{0,1:T(8,128)} async-done(((f32[128,7168]{0,1:T(8,128)}), f32[128,448]{0,1:T(8,128)}) %reduce-scatter.6.cloned.1.call-update) | async-done | bytes 229392 | tf_op jit(solution)/shard_map/reduce_scatter | solution.py:67
  124.6 211.9 %reduce-scatter.4.cloned.1.call-done = f32[128,448]{0,1:T(8,128)} async-done(((f32[2048,448]{0,1:T(8,128)}), f32[128,448]{0,1:T(8,128)}) %reduce-scatter.4.cloned.1.call-update) | async-done | bytes 229392 | tf_op jit(solution)/shard_map/reduce_scatter | solution.py:55
  336.5 1.8 fusion.39
  338.3 0.0 all-gather.6.cloned.1.call-update
  338.3 0.0 all-gather.8.cloned.1.call-start
  338.3 31.5 %psum.22 = f32[128]{0:T(128)S(1)} all-reduce(f32[128]{0:T(128)S(1)} %get-tuple-element.10), channel_id=1, replica_groups=mesh['section'=16,'mp'=16] {'mp'}, use_global_device_ids=true, to_apply=%region_7.8 | all-reduce | flops 128 | bytes 1024 | tf_op jit(solution)/shard_map/psum | solution.py:69
  369.8 7.1 all-gather.6.cloned.1.call-done
  376.9 2.5 fusion.2
  379.4 0.0 copy-done.4
  379.4 1.8 fusion.37
  381.2 0.0 all-gather.8.cloned.1.call-update
  381.2 0.0 reduce-scatter.8.cloned.1.call-start
  381.3 0.1 broadcast_bitcast_fusion
  381.4 77.8 %all-gather.8.cloned.1.call-done = bf16[2048,448]{0,1:T(8,128)(2,1)} async-done(((bf16[128,448]{0,1:T(8,128)(2,1)}), bf16[2048,448]{0,1:T(8,128)(2,1)}) %all-gather.8.cloned.1.call-update) | async-done | bytes 1835024 | tf_op jit(solution)/shard_map/all_gather | solution.py:76
  459.1 1.7 copy.69
  460.8 1.9 gather_fusion.1
  462.7 1.9 copy.53
  464.6 0.7 copy-done.2
  465.3 0.7 fusion.10
  465.9 32.0 %psum.23 = f32[2048]{0:T(1024)S(1)} all-reduce(f32[2048]{0:T(1024)S(1)} %fusion.10), channel_id=1, replica_groups=mesh['section'=16,'mp'=16] {'mp'}, use_global_device_ids=true, to_apply=%region_9.10 | all-reduce | flops 2048 | bytes 16384 | tf_op jit(solution)/shard_map/psum | solution.py:85
  498.0 6.7 fusion
  504.6 2.2 copy.46
  506.8 6.1 fusion.44
  512.9 0.0 reduce-scatter.8.cloned.1.call-update
  513.0 0.0 copy-start.1
  513.0 6.1 fusion.27
  519.1 213.5 %reduce-scatter.8.cloned.1.call-done = f32[12,16,448]{2,0,1:T(8,128)} async-done(((f32[12,256,448]{2,0,1:T(8,128)}), f32[12,16,448]{2,0,1:T(8,128)}) %reduce-scatter.8.cloned.1.call-update) | async-done | bytes 344080 | tf_op jit(solution)/shard_map/reduce_scatter | solution.py:96
  732.6 1.1 convert_element_type.54
  733.7 0.8 copy.45
  734.5 0.0 copy-done.1
  (13 shorter events, 0.1 us)
Async XLA Ops:
  7.2 14.8 %copy-start = (bf16[12,256,448]{1,2,0:T(8,128)(2,1)S(1)}, bf16[12,256,448]{1,2,0:T(8,128)(2,1)}, u32[]{:S(2)}) copy-start(bf16[12,256,448]{1,2,0:T(8,128)(2,1)} %param.14) | copy-start | bytes 8257540
  7.2 49.4 %all-gather.4.cloned.1.call-start = ((), (), s32[]{:S(2)}) async-start(), calls=%async_computation.3 | async-start | bytes 4456448 | tf_op jit(solution)/shard_map/all_gather | solution.py:40
  12.6 112.0 %reduce-scatter.6.cloned.1.call-start = ((), (), s32[]{:S(2)}) async-start(), calls=%async_computation.6 | async-start | bytes 3899392 | tf_op jit(solution)/shard_map/reduce_scatter | solution.py:67
  20.4 0.7 copy-start.5
  20.4 316.1 %reduce-scatter.4.cloned.1.call-start = ((), (), s32[]{:S(2)}) async-start(), calls=%async_computation.4 | async-start | bytes 3899392 | tf_op jit(solution)/shard_map/reduce_scatter | solution.py:55
  24.6 39.5 %copy-start.3 = (bf16[4,256,448]{1,0,2:T(4,128)(2,1)S(1)}, bf16[4,256,448]{1,0,2:T(4,128)(2,1)}, u32[]{:S(2)}) copy-start(bf16[4,256,448]{1,0,2:T(4,128)(2,1)} %fusion.23) | copy-start | bytes 2752516
  111.6 0.7 copy-start.6
  111.6 267.8 %copy-start.4 = (bf16[128,448]{0,1:T(8,128)(2,1)S(1)}, bf16[128,448]{0,1:T(8,128)(2,1)}, u32[]{:S(2)}) copy-start(bf16[128,448]{0,1:T(8,128)(2,1)} %param.19) | copy-start | bytes 344068
  111.6 265.3 %all-gather.6.cloned.1.call-start = ((), (), s32[]{:S(2)}) async-start(), calls=%async_computation.5 | async-start | bytes 1949696 | tf_op jit(solution)/shard_map/all_gather | solution.py:57
  338.3 120.8 %all-gather.8.cloned.1.call-start = ((), (), s32[]{:S(2)}) async-start(), calls=%async_computation.7 | async-start | bytes 1949696 | tf_op jit(solution)/shard_map/all_gather | solution.py:76
  381.2 351.4 %reduce-scatter.8.cloned.1.call-start = ((), (), s32[]{:S(2)}) async-start(), calls=%async_computation.8 | async-start | bytes 8912896 | tf_op jit(solution)/shard_map/reduce_scatter | solution.py:96
  462.7 2.6 copy-start.2
  513.0 221.5 %copy-start.1 = (bf16[12,256,448]{1,2,0:T(8,128)(2,1)S(1)}, bf16[12,256,448]{1,2,0:T(8,128)(2,1)}, u32[]{:S(2)}) copy-start(bf16[12,256,448]{1,2,0:T(8,128)(2,1)} %param.14) | copy-start | bytes 8257540
Sparse Core Ops, SparseCore 0:
  12.7 43.8 all-gather.3
  59.1 65.4 reduce-scatter.5
  128.6 207.8 reduce-scatter.3
  338.8 38.1 all-gather.5
  381.3 77.7 all-gather.7
  513.1 219.4 reduce-scatter.7
where the time goes:
time: 745 us; the launch traced here: 741 us
  waiting for transfers between devices  555 us (74%)
  blocking collectives  90.8 us (12%)
  matrix products  37.8 us (5%)
  local copies, waits for them, and re-layouts  30.6 us (4%)
  between operations  14.3 us (2%)
  other arithmetic  13.2 us (2%)
    reduce_scatter x1, waiting for transfers between devices, body(): lax.psum_scatter(per_band, 'section', scatter_dimension=1, tiled=True)  214 us
    reduce_scatter x1, waiting for transfers between devices, body(): lax.psum_scatter(reordered, 'section', scatter_dimension=0, tiled=True)  212 us
    all_gather x1, waiting for transfers between devices, body(): all_grads = lax.all_gather(input_grad, 'section', axis=0, tiled=True)  77.8 us
    psum x1, blocking collectives, body(): lax.psum(jnp.sum(group_out * unit_grad, axis=1), 'mp') / model_width  32 us
    all_gather x1, waiting for transfers between devices, body(): gathered = lax.all_gather(chosen, 'mp', axis=0, tiled=True)  31.9 us
    psum x1, blocking collectives, body(): lax.psum(jnp.sum(own_rows * gain_cols[None, :] * grad_cols, axis=1), 'mp')  31.5 us
    psum x1, blocking collectives, body(): square_sums = lax.psum(jnp.sum(group_out * group_out, axis=1), 'mp')  27.3 us
  transfers between devices with their start and end apart: 6, of which 6 were waited for; matrix products, arithmetic and copies ran while one was open for 6% of the time, Pallas kernels for 0%

commit v1 on v0

v1 whole, which is shorter than its diff:
```python
import functools

import jax
import jax.numpy as jnp
from jax import lax
from jax.experimental import pallas as pl
from jax.experimental.pallas import tpu as pltpu
from jax.sharding import PartitionSpec as P

EPSILON = 1e-05
MESH = pl.DeviceIdType.MESH
F32 = jnp.float32
BF16 = jnp.bfloat16
NEAR = 8
TILE = 16


def kernel(
    model_width,
    pick_ref,
    count_ref,
    plan_ref,
    pix_ref,
    gain_ref,
    tg_ref,
    qc_ref,
    rc_ref,
    w_hbm,
    wq_hbm,
    q_ref,
    bg_ref,
    live,
    member,
    w_ref,
    wq_ref,
    cand,
    xg,
    stage,
    crecv,
    p_ref,
    go,
    sums,
    table,
    ps1,
    ps2,
    ag,
    tgng,
    gb,
    pb,
    cr,
    ybuf,
    yrecv,
    acc,
    local_sem,
    cand_send,
    cand_recv,
    x_send,
    x_recv,
    c_send,
    c_recv,
    p1_send,
    p1_recv,
    p2_send,
    p2_recv,
    ag_send,
    ag_recv,
    cr_send,
    cr_recv,
    y_send,
    y_recv,
):
    groups, slots = pick_ref.shape
    bands = w_ref.shape[0]
    peers = xg.shape[0]
    tokens, cols = qc_ref.shape
    chunks = tokens // TILE
    me = lax.axis_index("mp")
    section = lax.axis_index("section")
    half = section // NEAR
    ring = lax.rem(section, NEAR)
    low = lax.rem(section, 4)
    block = section // 4

    copy_wq = pltpu.make_async_copy(wq_hbm, wq_ref, local_sem.at[0])
    copy_w = pltpu.make_async_copy(w_hbm, w_ref, local_sem.at[1])
    copy_wq.start()
    copy_w.start()

    def peer(i):
        return lax.rem(me + i, peers)

    def at_ring(step):
        return half * NEAR + lax.rem(ring + step + NEAR, NEAR)

    down, up = at_ring(-1), at_ring(1)
    across = (1 - half) * NEAR + ring

    barrier = pltpu.get_barrier_semaphore()

    @pl.loop(1, peers)
    def _(i):
        pl.semaphore_signal(barrier, inc=1, device_id={"mp": peer(i)}, device_id_type=MESH)

    for other in (down, up, across):
        pl.semaphore_signal(barrier, inc=1, device_id={"section": other}, device_id_type=MESH)
    pl.semaphore_wait(barrier, peers - 1 + 3)

    def cand_copy(i):
        to = peer(i)
        return pltpu.make_async_remote_copy(
            src_ref=pix_ref.at[to],
            dst_ref=cand.at[me // 4],
            send_sem=cand_send.at[i],
            recv_sem=cand_recv.at[me // 4],
            device_id={"mp": to},
            device_id_type=MESH,
        )

    owner = lax.rem(me, 4) == low
    own_piece = pltpu.make_async_copy(pix_ref.at[me], cand.at[me // 4], cand_recv.at[me // 4])

    @pl.when(owner)
    def _():
        own_piece.start()

        @pl.loop(1, peers)
        def _(i):
            cand_copy(i).start()

    table[...] = jnp.zeros_like(table)

    @pl.loop(0, groups)
    def _(g):
        used = count_ref[g]
        for k in range(slots):
            live[g, k] = jnp.where(k < used, 1.0, 0.0).astype(F32)
        for b in range(bands):
            hit = jnp.float32(0.0)
            for k in range(slots):
                same = jnp.logical_and(pick_ref[g, k] == b, k < used)
                hit = hit + jnp.where(same, 1.0, 0.0).astype(F32)
            member[g, b] = hit

    copy_wq.wait()

    @pl.loop(0, peers)
    def _(j):
        rows = pl.ds(pl.multiple_of(j * cols, 64), cols)
        stage[j] = lax.dot_general(
            qc_ref[...], wq_ref[rows, :], (((1,), (1,)), ((), ())), preferred_element_type=F32
        ).astype(BF16)

    for c in range(4):
        pltpu.make_async_copy(pix_ref.at[0], cand.at[c], cand_recv.at[c]).wait()

    xg[me] = cand[plan_ref[block]]

    def send_own(buf, send, recv):
        def at(i):
            return pltpu.make_async_remote_copy(
                src_ref=buf.at[me],
                dst_ref=buf.at[me],
                send_sem=send.at[i],
                recv_sem=recv.at[me],
                device_id={"mp": peer(i)},
                device_id_type=MESH,
            )

        @pl.loop(1, peers)
        def _(i):
            at(i).start()

    def wait_recv(buf, recv):
        @pl.loop(1, peers)
        def _(i):
            src = peer(i)
            pltpu.make_async_copy(buf.at[src], buf.at[src], recv.at[src]).wait()

    def wait_send(buf, send):
        @pl.loop(1, peers)
        def _(i):
            pltpu.make_async_copy(buf.at[me], buf.at[me], send.at[i]).wait()

    send_own(xg, x_send, x_recv)

    @pl.loop(1, peers)
    def _(i):
        to = peer(i)
        pltpu.make_async_remote_copy(
            src_ref=stage.at[to],
            dst_ref=crecv.at[me],
            send_sem=c_send.at[i],
            recv_sem=c_recv.at[me],
            device_id={"mp": to},
            device_id_type=MESH,
        ).start()

    crecv[me] = stage[me]
    copy_w.wait()
    wait_recv(xg, x_recv)

    half_bands = bands // 2

    def band_pixels(b):
        side = b // half_bands
        start = pl.multiple_of(lax.rem(b, half_bands) * TILE, TILE)
        return jnp.concatenate(
            [xg[2 * i + side, pl.ds(start, TILE), :] for i in range(peers // 2)], axis=0
        )

    @pl.loop(0, bands)
    def _(b):
        p_ref[b] = jnp.dot(band_pixels(b), w_ref[b], preferred_element_type=F32)

    lane = lax.broadcasted_iota(jnp.int32, (TILE, 128), 1)

    def put(stat, at, value):
        return jnp.where(lane == at, jnp.sum(value, axis=1, keepdims=True), stat)

    @pl.loop(0, chunks)
    def _(r):
        rows = pl.ds(pl.multiple_of(r * TILE, TILE), TILE)
        stat = jnp.zeros((TILE, 128), F32)
        resid = rc_ref[rows, :].astype(F32)
        for g in range(groups):
            out = live[g, 0] * p_ref[pick_ref[g, 0], rows, :]
            for k in range(1, slots):
                out = out + live[g, k] * p_ref[pick_ref[g, k], rows, :]
            go[g, rows, :] = out
            stat = put(stat, g, out * out)
            stat = put(stat, groups + g, out * gain_ref[g : g + 1, :] * resid)
        sums[rows, :] = stat

    ps1[me] = sums[...].T[: ps1.shape[1], :]
    send_own(ps1, p1_send, p1_recv)
    wait_recv(ps1, p1_recv)

    def total(buf):
        value = buf[0]
        for i in range(1, peers):
            value = value + buf[i]
        return value

    first = total(ps1)
    scale = lax.rsqrt(first[:groups] / model_width + EPSILON)
    table[0:groups, :] = scale
    sums[...] = table[...].T

    @pl.loop(0, chunks)
    def _(r):
        rows = pl.ds(pl.multiple_of(r * TILE, TILE), TILE)
        col = sums[rows, :]
        value = jnp.zeros((TILE, cols), F32)
        for g in range(groups):
            value = value + go[g, rows, :] * col[:, g : g + 1] * gain_ref[g : g + 1, :]
        ag[me, rows, :] = value.astype(BF16)

    wait_recv(crecv, c_recv)
    own_gain = tg_ref[pl.ds(me, 1), :]

    @pl.loop(0, chunks)
    def _(r):
        rows = pl.ds(pl.multiple_of(r * TILE, TILE), TILE)
        grad = crecv[0, rows, :].astype(F32)
        for i in range(1, peers):
            grad = grad + crecv[i, rows, :].astype(F32)
        grad = grad * own_gain
        tgng[rows, :] = grad
        trunk = ag[me, rows, :].astype(F32)
        stat = jnp.zeros((TILE, 128), F32)
        stat = put(stat, 2 * groups, trunk * trunk)
        stat = put(stat, 2 * groups + 1, trunk * grad)
        for g in range(groups):
            unit = go[g, rows, :] * gain_ref[g : g + 1, :]
            stat = put(stat, g, unit * grad)
            stat = put(stat, groups + g, unit * trunk)
        sums[rows, :] = stat

    ps2[me] = sums[...].T[: ps2.shape[1], :]
    send_own(ps2, p2_send, p2_recv)
    send_own(ag, ag_send, ag_recv)
    wait_recv(ps2, p2_recv)
    second = total(ps2)
    row_scale = lax.rsqrt(second[2 * groups : 2 * groups + 1] / model_width + EPSILON)
    row_stat = second[2 * groups + 1 : 2 * groups + 2] / model_width
    cube_stat = row_scale * row_scale * row_scale * row_stat
    group_stat = (
        first[groups : 2 * groups]
        + row_scale * second[:groups]
        - cube_stat * second[groups : 2 * groups]
    ) / model_width
    table[groups : 2 * groups, :] = scale * scale * scale * group_stat
    table[2 * groups : 2 * groups + 1, :] = row_scale
    table[2 * groups + 1 : 2 * groups + 2, :] = cube_stat
    sums[...] = table[...].T

    @pl.loop(0, chunks)
    def _(r):
        rows = pl.ds(pl.multiple_of(r * TILE, TILE), TILE)
        col = sums[rows, :]
        trunk = ag[me, rows, :].astype(F32)
        grad = (
            rc_ref[rows, :].astype(F32)
            + col[:, 2 * groups : 2 * groups + 1] * tgng[rows, :]
            - col[:, 2 * groups + 1 : 2 * groups + 2] * trunk
        )
        grad = grad.astype(BF16).astype(F32)
        for g in range(groups):
            go[g, rows, :] = (
                col[:, g : g + 1] * (grad * gain_ref[g : g + 1, :])
                - go[g, rows, :] * col[:, groups + g : groups + g + 1]
            )
        for b0 in range(0, bands, 3):
            found = [jnp.zeros((TILE, cols), F32) for _ in range(3)]
            for g in range(groups):
                value = go[g, rows, :]
                found = [found[d] + member[g, b0 + d] * value for d in range(3)]
            for d in range(3):
                gb[b0 + d, rows, :] = found[d].astype(BF16)

    @pl.loop(0, bands)
    def _(b):
        value = lax.dot_general(
            band_pixels(b), gb[b], (((0,), (0,)), ((), ())), preferred_element_type=F32
        )
        rows = pl.ds(pl.multiple_of(b * TILE, TILE), TILE)
        pb[:, rows, :] = value.reshape(pb.shape[0], TILE, cols).astype(BF16)

    def unit(way, h, t):
        offset = (4 - t) if way else (t - 4)
        return h * NEAR + lax.rem(ring + offset + NEAR, NEAR)

    def link(way, h, t):
        return pltpu.make_async_remote_copy(
            src_ref=pb.at[unit(way, h, t)],
            dst_ref=cr.at[way, h, t],
            send_sem=cr_send.at[way, h, t],
            recv_sem=cr_recv.at[way, h, t],
            device_id={"section": up if way else down},
            device_id_type=MESH,
        )

    for way, h, t in ((0, 0, 0), (1, 1, 0), (0, 1, 1), (1, 0, 1)):
        link(way, h, t).start()

    def advance(way, h, t):
        link(way, h, t - 1).wait_recv()
        at = unit(way, h, t)
        pb[at] = (pb[at].astype(F32) + cr[way, h, t - 1].astype(F32)).astype(BF16)
        link(way, h, t).start()

    advance(0, 0, 1)
    advance(1, 1, 1)
    advance(0, 1, 2)
    advance(1, 0, 2)

    wait_recv(ag, ag_recv)
    acc[...] = jnp.zeros_like(acc)
    scale_col = sums[:, 2 * groups : 2 * groups + 1]

    @pl.loop(0, peers)
    def _(j):
        rows = pl.ds(pl.multiple_of(j * cols, 64), cols)
        normed = (ag[j].astype(F32) * scale_col * tg_ref[pl.ds(j, 1), :]).astype(BF16)
        acc[...] += jnp.dot(normed, wq_ref[rows, :], preferred_element_type=F32)

    q_ref[...] = acc[...].astype(BF16)

    advance(0, 0, 2)
    advance(1, 1, 2)
    advance(0, 1, 3)
    advance(1, 0, 3)
    advance(0, 0, 3)
    advance(1, 1, 3)
    for way, h in ((0, 1), (1, 0), (0, 0), (1, 1)):
        link(way, h, 3).wait_recv()

    def gathered(h):
        return (
            pb[h * NEAR + ring].astype(F32)
            + cr[0, h, 3].astype(F32)
            + cr[1, h, 3].astype(F32)
        )

    ybuf[...] = gathered(1 - half).astype(BF16)
    over = pltpu.make_async_remote_copy(
        src_ref=ybuf,
        dst_ref=yrecv,
        send_sem=y_send,
        recv_sem=y_recv,
        device_id={"section": across},
        device_id_type=MESH,
    )
    over.start()
    over.wait_recv()
    bg_ref[...] = (gathered(half) + yrecv[...].astype(F32)).astype(BF16)

    over.wait_send()
    for way, h, t0 in ((0, 0, 0), (1, 1, 0), (0, 1, 1), (1, 0, 1)):
        for t in range(t0, 4):
            link(way, h, t).wait_send()

    @pl.when(owner)
    def _():
        @pl.loop(1, peers)
        def _(i):
            cand_copy(i).wait_send()

    wait_send(xg, x_send)
    wait_send(crecv, c_send)
    wait_send(ps1, p1_send)
    wait_send(ps2, p2_send)
    wait_send(ag, ag_send)


def body(
    pixels,
    band_pick,
    band_count,
    tok_gain,
    bands_weight,
    plan,
    trunk_gain,
    query_weight,
    query_cot,
    resid_cot,
):
    peers = lax.axis_size("mp")
    sections = lax.axis_size("section")
    groups = band_pick.shape[0]
    tokens, bands, patch = pixels.shape
    cols = bands_weight.shape[2]
    model_width = cols * peers
    piece = tokens * bands // peers
    pieces = (
        pixels.reshape(tokens // TILE, TILE, bands, patch)
        .transpose(0, 2, 1, 3)
        .reshape(peers, piece, patch)
    )
    rows = bands * patch // sections
    vmem = pl.BlockSpec(memory_space=pltpu.VMEM)
    smem = pl.BlockSpec(memory_space=pltpu.SMEM)
    hbm = pl.BlockSpec(memory_space=pl.ANY)
    dma = pltpu.SemaphoreType.DMA
    queries, grads = pl.pallas_call(
        functools.partial(kernel, model_width),
        out_shape=(
            jax.ShapeDtypeStruct((tokens, cols), BF16),
            jax.ShapeDtypeStruct((rows, cols), BF16),
        ),
        in_specs=[smem] * 3 + [vmem] * 5 + [hbm] * 2,
        out_specs=(vmem, vmem),
        scratch_shapes=[
            pltpu.SMEM((groups, band_pick.shape[1]), F32),
            pltpu.SMEM((groups, bands), F32),
            pltpu.VMEM(bands_weight.shape, BF16),
            pltpu.VMEM(query_weight.shape, BF16),
            pltpu.VMEM((4, piece, patch), BF16),
            pltpu.VMEM((peers, piece, patch), BF16),
            pltpu.VMEM((peers, tokens, cols), BF16),
            pltpu.VMEM((peers, tokens, cols), BF16),
            pltpu.VMEM((bands, tokens, cols), F32),
            pltpu.VMEM((groups, tokens, cols), F32),
            pltpu.VMEM((tokens, 128), F32),
            pltpu.VMEM((128, tokens), F32),
            pltpu.VMEM((peers, 2 * groups, tokens), F32),
            pltpu.VMEM((peers, 2 * groups + 8, tokens), F32),
            pltpu.VMEM((peers, tokens, cols), BF16),
            pltpu.VMEM((tokens, cols), F32),
            pltpu.VMEM((bands, tokens, cols), BF16),
            pltpu.VMEM((sections, rows, cols), BF16),
            pltpu.VMEM((2, 2, 4, rows, cols), BF16),
            pltpu.VMEM((rows, cols), BF16),
            pltpu.VMEM((rows, cols), BF16),
            pltpu.VMEM((tokens, cols), F32),
            dma((2,)),
            dma((peers,)),
            dma((4,)),
        ]
        + [dma((peers,))] * 10
        + [dma((2, 2, 4)), dma((2, 2, 4)), dma, dma],
        compiler_params=pltpu.CompilerParams(
            collective_id=0, has_side_effects=True, vmem_limit_bytes=60 * 1024 * 1024
        ),
    )(
        band_pick,
        band_count,
        plan,
        pieces,
        tok_gain,
        trunk_gain.reshape(peers, cols),
        query_cot,
        resid_cot,
        bands_weight,
        query_weight,
    )
    return (queries, grads.reshape(bands, rows // bands, cols))


def solution(mesh):
    placed = (
        P("mp", None, None),
        P(),
        P(),
        P(None, "mp"),
        P(None, None, "mp"),
        P(),
        P(),
        P(None, "mp"),
        P("section", "mp"),
        P("section", "mp"),
    )
    return jax.shard_map(
        body,
        mesh=mesh,
        in_specs=placed,
        out_specs=(P("section", "mp"), P(None, "section", "mp")),
        check_vma=False,
    )
```

time: 745 us -> 163 us (0.22)
  waiting for transfers between devices: 555 us -> 0 us
  Pallas kernels: 0 us -> 136 us
  blocking collectives: 90.8 us -> 0 us
  matrix products: 37.8 us -> 0 us
  between operations: 14.3 us -> 0.64 us
  other arithmetic: 13.2 us -> 0 us
    reduce_scatter x3 -> x0, waiting for transfers between devices: 438 us -> none  [the longest x1 214 us: body(): lax.psum_scatter(per_band, 'section', scatter_dimension=1, tiled=True)]
    pallas_call x0 -> x1, Pallas kernels: none -> 136 us  [body(): pl.pallas_call(functools.partial(kernel, model_width), out_shape=(jax.Sha...]
    all_gather x3 -> x0, waiting for transfers between devices: 117 us -> none  [the longest x1 77.8 us: body(): all_grads = lax.all_gather(input_grad, 'section', axis=0, tiled=True)]
    psum x3 -> x0, blocking collectives: 90.8 us -> none  [the longest x1 32 us: body(): lax.psum(jnp.sum(group_out * unit_grad, axis=1), 'mp') / model_width]
    dot_general x7 -> x0, matrix products: 37.8 us -> none  [the longest x1 7.77 us: body(): lax.dot_general(query_cot, query_weight, (((1,), (1,)), ((), ())), prefer...]
    unnamed x19 -> x7, local copies, waits for them, and re-layouts: 2.92 us -> 22.5 us
    gather x4 -> x0, local copies, waits for them, and re-layouts: 10.9 us -> none  [the longest x2 7.12 us: body(): jnp.take(group_term.reshape(micro_count, micro_rows, cols_dev), plan, axi...]
    all_gather x1 -> x0, local copies, waits for them, and re-layouts: 7.55 us -> none  [body(): gathered = lax.all_gather(chosen, 'mp', axis=0, tiled=True)]
  transfers between devices with their start and end apart: 6 -> 0, of which waited for: 6 -> 0; matrix products, arithmetic and copies ran while one was open for 6% -> 0% of each run, Pallas kernels for 0% -> 0%
where the time goes in v1:
time: 163 us; the launch traced here: 162 us
  Pallas kernels  136 us (83%)
  local copies, waits for them, and re-layouts  26 us (16%)
    pallas_call x1, Pallas kernels, body(): pl.pallas_call(functools.partial(kernel, model_width), out_shape=(jax.Sha...  136 us
    unnamed x7, local copies, waits for them, and re-layouts  22.5 us

profile of v1, /device:TPU:1, one launch (start us, length us, event | category | flops | bytes accessed | tf_op | source)
XLA Modules:
  0.0 162.2 jit_solution(7522052043618113808)
XLA Ops:
  0.6 1.3 copy.13.pick_ref
  2.0 1.4 reshape.18.tg_ref
  3.4 1.7 %copy.14.qc_ref = bf16[128,448]{1,0:T(8,128)(2,1)} copy(bf16[128,448]{0,1:T(8,128)(2,1)} %param.18) | data formatting | bytes 229376 | tf_op args[8]
  5.1 1.7 %copy.15.rc_ref = bf16[128,448]{1,0:T(8,128)(2,1)} copy(bf16[128,448]{0,1:T(8,128)(2,1)} %param.19) | data formatting | bytes 229376 | tf_op args[9]
  6.7 2.1 %copy.12 = bf16[8,16,12,256]{3,1,2,0:T(8,128)(2,1)} copy(bf16[8,16,12,256]{3,1,0,2:T(8,128)(2,1)} %bitcast.6) | data formatting | bytes 1572864 | tf_op jit(solution)/shard_map/reshape | solution.py:436
  8.8 4.6 %copy.16.w_hbm = bf16[12,256,448]{2,1,0:T(8,128)(2,1)} copy(bf16[12,256,448]{1,2,0:T(8,128)(2,1)} %param.14) | data formatting | bytes 5505024 | tf_op args[4]
  13.4 9.9 %copy.17.wq_hbm = bf16[7168,448]{1,0:T(8,128)(2,1)} copy(bf16[7168,448]{0,1:T(8,128)(2,1)} %param.17) | data formatting | bytes 12845056 | tf_op args[7]
  23.3 135.6 %shard_map.113 = (bf16[128,448]{1,0:T(8,128)(2,1)}, bf16[192,448]{1,0:T(8,128)(2,1)}) custom-call(s32[16,4]{1,0:T(8,128)} %copy.13.pick_ref, s32[16]{0:T(128)} %count_ref.1, s32[4]{0:T(128)} %plan_ref.1, bf16[16,96,256]{2,1,0:T(8,128)(2,1)} %bitcast.5, f32[16,448]{1,0:T(8,128)} %gain_ref.1, f32[16,448]{1,0:T(8,128)} %reshape.18.tg_ref, ...), custom_call_target="tpu_custom_call" | custom-call | tf_op jit(solution)/shard_map/pallas_call | solution.py:445
  158.9 1.7 %copy.18 = bf16[128,448]{0,1:T(8,128)(2,1)} copy(bf16[128,448]{1,0:T(8,128)(2,1)} %get-tuple-element.6) | data formatting | bytes 229376
  160.6 1.6 copy.20

commit v2 on v1

v2 whole, which is shorter than its diff:
```python
import functools

import jax
import jax.numpy as jnp
from jax import lax
from jax.experimental import pallas as pl
from jax.experimental.pallas import tpu as pltpu
from jax.sharding import PartitionSpec as P

EPSILON = 1e-05
MESH = pl.DeviceIdType.MESH
F32 = jnp.float32
BF16 = jnp.bfloat16
NEAR = 8
TILE = 16
STEP = 112


def kernel(
    model_width,
    pick_ref,
    count_ref,
    plan_ref,
    pix_ref,
    gain_ref,
    tg_ref,
    qc_ref,
    rc_ref,
    w_hbm,
    wq_hbm,
    q_ref,
    bg_ref,
    live,
    member,
    w_ref,
    wq_ref,
    qc_rows,
    gain_wide,
    tg_wide,
    cand,
    xg,
    xt,
    stage,
    pre,
    crecv,
    p_ref,
    go,
    rows1,
    rows2,
    ps1,
    ps2,
    ag,
    tgng,
    gb,
    pb,
    cr,
    ybuf,
    yrecv,
    acc,
    local_sem,
    cand_send,
    cand_recv,
    x_send,
    x_recv,
    x_pass,
    pre_send,
    pre_recv,
    c_send,
    c_recv,
    p1_send,
    p1_recv,
    p2_send,
    p2_recv,
    ag_send,
    ag_recv,
    ag_pass,
    cr_send,
    cr_recv,
    y_send,
    y_recv,
):
    slots, groups = pick_ref.shape
    bands, tokens, patch = xg.shape
    cols = qc_ref.shape[0]
    peers = ag.shape[0]
    chips = peers // 2
    half_bands = bands // 2
    me = lax.axis_index("mp")
    chip = me // 2
    core = lax.rem(me, 2)
    twin = me + 1 - 2 * core
    section = lax.axis_index("section")
    half = section // NEAR
    ring = lax.rem(section, NEAR)
    low = lax.rem(section, 4)
    block = section // 4

    copy_wq = pltpu.make_async_copy(wq_hbm, wq_ref, local_sem.at[0])
    copy_w = pltpu.make_async_copy(w_hbm, w_ref, local_sem.at[1])
    copy_wq.start()
    copy_w.start()

    def peer(i):
        return lax.rem(me + i, peers)

    def near(i):
        return lax.rem(chip + i, chips)

    def at_ring(step):
        return half * NEAR + lax.rem(ring + step + NEAR, NEAR)

    down, up = at_ring(-1), at_ring(1)
    across = (1 - half) * NEAR + ring

    barrier = pltpu.get_barrier_semaphore()

    @pl.loop(1, peers)
    def _(i):
        pl.semaphore_signal(barrier, inc=1, device_id={"mp": peer(i)}, device_id_type=MESH)

    for other in (down, up, across):
        pl.semaphore_signal(barrier, inc=1, device_id={"section": other}, device_id_type=MESH)

    def remote(src, dst, send, recv, axis, to):
        return pltpu.make_async_remote_copy(
            src_ref=src,
            dst_ref=dst,
            send_sem=send,
            recv_sem=recv,
            device_id={axis: to},
            device_id_type=MESH,
        )

    @pl.loop(0, groups)
    def _(g):
        used = count_ref[g]
        for k in range(slots):
            live[g, k] = jnp.where(k < used, 1.0, 0.0).astype(F32)
        for b in range(bands):
            hit = jnp.float32(0.0)
            for k in range(slots):
                same = jnp.logical_and(pick_ref[k, g] == b, k < used)
                hit = hit + jnp.where(same, 1.0, 0.0).astype(F32)
            member[g, b] = hit

    qc_rows[...] = qc_ref[...].T
    pl.semaphore_wait(barrier, peers - 1 + 3)

    def piece(ref, j):
        start = pl.multiple_of((j // 2) * TILE, TILE)
        return ref.at[pl.ds(lax.rem(j, 2) * half_bands, half_bands), pl.ds(start, TILE), :]

    def cand_copy(i):
        to = peer(i)
        slot = me // 4
        return remote(
            piece(pix_ref, to), cand.at[slot], cand_send.at[i], cand_recv.at[slot], "mp", to
        )

    owner = lax.rem(me, 4) == low

    @pl.when(owner)
    def _():
        pltpu.make_async_copy(piece(pix_ref, me), cand.at[me // 4], cand_recv.at[me // 4]).start()

        @pl.loop(1, peers)
        def _(i):
            cand_copy(i).start()

    copy_wq.wait()

    def pre_copy(k):
        return remote(
            stage.at[2 * k + 1 - core], pre.at[k], pre_send.at[k], pre_recv.at[k], "mp", twin
        )

    @pl.loop(0, chips)
    def _(k):
        at = pl.ds(pl.multiple_of(k * 2 * cols, 128), 2 * cols)
        tiles = jnp.dot(qc_rows[...], wq_ref[:, at], preferred_element_type=F32).T
        stage[2 * k] = tiles[:cols].astype(BF16)
        stage[2 * k + 1] = tiles[cols:].astype(BF16)
        pre_copy(k).start()

    for c in range(4):
        pltpu.make_async_copy(cand.at[c], cand.at[c], cand_recv.at[c]).wait()

    def spread(view, send, recv):
        own = view(me)
        remote(own, own, send.at[0], recv.at[me], "mp", twin).start()

        @pl.loop(1, chips)
        def _(i):
            remote(own, own, send.at[i], recv.at[me], "mp", 2 * near(i) + core).start()

    def spread_wait(view, recv, hand):
        @pl.loop(1, chips)
        def _(i):
            src = 2 * near(i) + core
            block_of = view(src)
            pltpu.make_async_copy(block_of, block_of, recv.at[src]).wait()
            remote(block_of, block_of, hand.at[i], recv.at[src], "mp", twin).start()

        @pl.loop(0, chips)
        def _(i):
            src = 2 * near(i) + 1 - core
            block_of = view(src)
            pltpu.make_async_copy(block_of, block_of, recv.at[src]).wait()

    def spread_end(view, send, hand):
        own = view(me)

        @pl.loop(0, chips)
        def _(i):
            pltpu.make_async_copy(own, own, send.at[i]).wait()

        @pl.loop(1, chips)
        def _(i):
            pltpu.make_async_copy(own, own, hand.at[i]).wait()

    def x_view(j):
        return piece(xg, j)

    mine = pl.ds(pl.multiple_of(chip * TILE, TILE), TILE)
    xg[pl.ds(core * half_bands, half_bands), mine, :] = cand[plan_ref[block]]
    spread(x_view, x_send, x_recv)

    def cross_copy(i):
        k = near(i)
        return remote(
            stage.at[2 * k + core], crecv.at[chip], c_send.at[i], c_recv.at[chip], "mp", 2 * k + core
        )

    @pl.loop(1, chips)
    def _(i):
        k = near(i)
        pltpu.make_async_copy(pre.at[k], pre.at[k], pre_recv.at[k]).wait()
        stage[2 * k + core] = (stage[2 * k + core].astype(F32) + pre[k].astype(F32)).astype(BF16)
        cross_copy(i).start()

    pltpu.make_async_copy(pre.at[chip], pre.at[chip], pre_recv.at[chip]).wait()
    crecv[chip] = (stage[2 * chip + core].astype(F32) + pre[chip].astype(F32)).astype(BF16)

    gain_cols = gain_ref[...].T
    for g in range(groups):
        gain_wide[g] = jnp.broadcast_to(gain_cols[:, g : g + 1], (cols, tokens))
    tg_cols = tg_ref[...].T
    for k in range(tg_ref.shape[0]):
        tg_wide[128 * k : 128 * (k + 1), :] = jnp.broadcast_to(tg_cols[:, k : k + 1], (128, tokens))

    copy_w.wait()
    spread_wait(x_view, x_recv, x_pass)

    @pl.loop(0, bands)
    def _(b):
        p_ref[b] = lax.dot_general(
            w_ref[b], xg[b], (((1,), (1,)), ((), ())), preferred_element_type=F32
        )

    def fold(value):
        return jnp.sum(value.reshape(-1, 8, tokens), axis=0)

    def line(value):
        return jnp.sum(value, axis=0, keepdims=True)

    steps = range(0, cols, STEP)

    @pl.loop(0, groups)
    def _(g):
        square = jnp.zeros((8, tokens), F32)
        with_resid = jnp.zeros((8, tokens), F32)
        for d in steps:
            at = slice(d, d + STEP)
            out = live[g, 0] * p_ref[pick_ref[0, g], at, :]
            for k in range(1, slots):
                out = out + live[g, k] * p_ref[pick_ref[k, g], at, :]
            go[g, at, :] = out
            square = square + fold(out * out)
            with_resid = with_resid + fold(out * gain_wide[g, at, :] * rc_ref[at, :].astype(F32))
        rows1[pl.ds(g, 1), :] = line(square)
        rows1[pl.ds(groups + g, 1), :] = line(with_resid)

    def send_own(buf, send, recv):
        @pl.loop(1, peers)
        def _(i):
            remote(buf.at[me], buf.at[me], send.at[i], recv.at[me], "mp", peer(i)).start()

    def wait_recv(buf, recv):
        @pl.loop(1, peers)
        def _(i):
            src = peer(i)
            pltpu.make_async_copy(buf.at[src], buf.at[src], recv.at[src]).wait()

    def wait_send(buf, send):
        @pl.loop(1, peers)
        def _(i):
            pltpu.make_async_copy(buf.at[me], buf.at[me], send.at[i]).wait()

    def total(buf):
        value = buf[0]
        for i in range(1, peers):
            value = value + buf[i]
        return value

    ps1[me] = rows1[...]
    send_own(ps1, p1_send, p1_recv)

    @pl.loop(0, bands)
    def _(b):
        xt[b] = xg[b].T

    wait_recv(ps1, p1_recv)
    first = total(ps1)
    scale = lax.rsqrt(first[:groups] / model_width + EPSILON)

    for d in range(0, cols, 32):
        at = slice(d, d + 32)
        value = jnp.zeros((32, tokens), F32)
        for g in range(groups):
            value = value + go[g, at, :] * scale[g : g + 1, :] * gain_wide[g, at, :]
        ag[me, at, :] = value.astype(BF16)

    @pl.loop(1, chips)
    def _(i):
        k = near(i)
        pltpu.make_async_copy(crecv.at[k], crecv.at[k], c_recv.at[k]).wait()

    own_rows = pl.multiple_of(me * cols, 64)
    trunk_square = jnp.zeros((8, tokens), F32)
    trunk_grad = jnp.zeros((8, tokens), F32)
    for d in steps:
        at = slice(d, d + STEP)
        grad = crecv[0, at, :].astype(F32)
        for i in range(1, chips):
            grad = grad + crecv[i, at, :].astype(F32)
        grad = grad * tg_wide[pl.ds(own_rows + d, STEP), :]
        tgng[at, :] = grad
        trunk = ag[me, at, :].astype(F32)
        trunk_square = trunk_square + fold(trunk * trunk)
        trunk_grad = trunk_grad + fold(trunk * grad)
    rows2[2 * groups : 2 * groups + 1, :] = line(trunk_square)
    rows2[2 * groups + 1 : 2 * groups + 2, :] = line(trunk_grad)
    rows2[2 * groups + 2 :, :] = jnp.zeros((6, tokens), F32)

    @pl.loop(0, groups)
    def _(g):
        with_grad = jnp.zeros((8, tokens), F32)
        with_trunk = jnp.zeros((8, tokens), F32)
        for d in steps:
            at = slice(d, d + STEP)
            unit = go[g, at, :] * gain_wide[g, at, :]
            with_grad = with_grad + fold(unit * tgng[at, :])
            with_trunk = with_trunk + fold(unit * ag[me, at, :].astype(F32))
        rows2[pl.ds(g, 1), :] = line(with_grad)
        rows2[pl.ds(groups + g, 1), :] = line(with_trunk)

    ps2[me] = rows2[...]
    send_own(ps2, p2_send, p2_recv)

    def ag_view(j):
        return ag.at[j]

    spread(ag_view, ag_send, ag_recv)
    wait_recv(ps2, p2_recv)
    second = total(ps2)
    row_scale = lax.rsqrt(second[2 * groups : 2 * groups + 1] / model_width + EPSILON)
    row_stat = second[2 * groups + 1 : 2 * groups + 2] / model_width
    cube_stat = row_scale * row_scale * row_scale * row_stat
    group_stat = (
        first[groups : 2 * groups]
        + row_scale * second[:groups]
        - cube_stat * second[groups : 2 * groups]
    ) / model_width
    cube_group = scale * scale * scale * group_stat

    for d in range(0, cols, 32):
        at = slice(d, d + 32)
        grad = (
            rc_ref[at, :].astype(F32)
            + row_scale * tgng[at, :]
            - cube_stat * ag[me, at, :].astype(F32)
        )
        grad = grad.astype(BF16).astype(F32)
        for g in range(groups):
            go[g, at, :] = (
                scale[g : g + 1, :] * (grad * gain_wide[g, at, :])
                - go[g, at, :] * cube_group[g : g + 1, :]
            )

    @pl.loop(0, cols // 32)
    def _(r):
        at = pl.ds(pl.multiple_of(r * 32, 32), 32)
        for b0 in range(0, bands, 6):
            found = [jnp.zeros((32, tokens), F32) for _ in range(6)]
            for g in range(groups):
                value = go[g, at, :]
                found = [found[d] + member[g, b0 + d] * value for d in range(6)]
            for d in range(6):
                gb[b0 + d, at, :] = found[d].astype(BF16)

    @pl.loop(0, bands)
    def _(b):
        value = lax.dot_general(
            xt[b], gb[b], (((1,), (1,)), ((), ())), preferred_element_type=F32
        )
        rows = pl.ds(pl.multiple_of(b * TILE, TILE), TILE)
        pb[:, rows, :] = value.reshape(pb.shape[0], TILE, cols).astype(BF16)

    def unit(way, h, t):
        offset = (4 - t) if way else (t - 4)
        side = half if h else 1 - half
        return side * NEAR + lax.rem(ring + offset + NEAR, NEAR)

    def link(way, h, t):
        return remote(
            pb.at[unit(way, h, t)],
            cr.at[way, h, t],
            cr_send.at[way, h, t],
            cr_recv.at[way, h, t],
            "section",
            up if way else down,
        )

    for way, h, t in ((0, 0, 0), (1, 1, 0), (1, 0, 1), (0, 1, 1)):
        link(way, h, t).start()

    def advance(way, h, t):
        link(way, h, t - 1).wait_recv()
        at = unit(way, h, t)
        pb[at] = (pb[at].astype(F32) + cr[way, h, t - 1].astype(F32)).astype(BF16)
        link(way, h, t).start()

    advance(0, 0, 1)
    advance(1, 0, 2)
    advance(1, 1, 1)
    advance(0, 1, 2)

    spread_wait(ag_view, ag_recv, ag_pass)
    acc[...] = jnp.zeros_like(acc)

    @pl.loop(0, chips)
    def _(k):
        rows = pl.ds(pl.multiple_of(k * 2 * cols, 128), 2 * cols)
        trunk = ag[pl.ds(2 * k, 2)].reshape(2 * cols, tokens).astype(F32)
        normed = (trunk * row_scale * tg_wide[rows, :]).astype(BF16)
        acc[...] += jnp.dot(wq_ref[:, rows], normed, preferred_element_type=F32)

    q_ref[...] = acc[...].astype(BF16)

    advance(0, 0, 2)
    advance(1, 0, 3)
    advance(1, 1, 2)
    advance(0, 1, 3)
    advance(0, 0, 3)
    advance(1, 1, 3)

    def gathered(h):
        side = half if h else 1 - half
        link(1, h, 3).wait_recv()
        link(0, h, 3).wait_recv()
        return (
            pb[side * NEAR + ring].astype(F32) + cr[0, h, 3].astype(F32) + cr[1, h, 3].astype(F32)
        )

    ybuf[...] = gathered(0).astype(BF16)
    over = remote(ybuf, yrecv, y_send, y_recv, "section", across)
    over.start()
    own_sum = gathered(1)
    over.wait_recv()
    bg_ref[...] = (own_sum + yrecv[...].astype(F32)).astype(BF16)

    over.wait_send()
    for way, h, t0 in ((0, 0, 0), (1, 1, 0), (0, 1, 1), (1, 0, 1)):
        for t in range(t0, 4):
            link(way, h, t).wait_send()

    @pl.when(owner)
    def _():
        @pl.loop(1, peers)
        def _(i):
            cand_copy(i).wait_send()

    spread_end(x_view, x_send, x_pass)
    spread_end(ag_view, ag_send, ag_pass)

    @pl.loop(0, chips)
    def _(k):
        pre_copy(k).wait_send()

    @pl.loop(1, chips)
    def _(i):
        cross_copy(i).wait_send()

    wait_send(ps1, p1_send)
    wait_send(ps2, p2_send)


def body(
    pixels,
    band_pick,
    band_count,
    tok_gain,
    bands_weight,
    plan,
    trunk_gain,
    query_weight,
    query_cot,
    resid_cot,
):
    peers = lax.axis_size("mp")
    chips = peers // 2
    sections = lax.axis_size("section")
    groups = band_pick.shape[0]
    tokens, bands, patch = pixels.shape
    cols = bands_weight.shape[2]
    model_width = cols * peers
    rows = bands * patch // sections
    vmem = pl.BlockSpec(memory_space=pltpu.VMEM)
    smem = pl.BlockSpec(memory_space=pltpu.SMEM)
    hbm = pl.BlockSpec(memory_space=pl.ANY)
    dma = pltpu.SemaphoreType.DMA
    queries, grads = pl.pallas_call(
        functools.partial(kernel, model_width),
        out_shape=(
            jax.ShapeDtypeStruct((cols, tokens), BF16),
            jax.ShapeDtypeStruct((rows, cols), BF16),
        ),
        in_specs=[smem] * 3 + [vmem] * 5 + [hbm] * 2,
        out_specs=(vmem, vmem),
        scratch_shapes=[
            pltpu.SMEM((groups, band_pick.shape[1]), F32),
            pltpu.SMEM((groups, bands), F32),
            pltpu.VMEM((bands, cols, patch), BF16),
            pltpu.VMEM((cols, model_width), BF16),
            pltpu.VMEM((tokens, cols), BF16),
            pltpu.VMEM((groups, cols, tokens), F32),
            pltpu.VMEM((model_width, tokens), F32),
            pltpu.VMEM((4, bands // 2, TILE, patch), BF16),
            pltpu.VMEM((bands, tokens, patch), BF16),
            pltpu.VMEM((bands, patch, tokens), BF16),
            pltpu.VMEM((peers, cols, tokens), BF16),
            pltpu.VMEM((chips, cols, tokens), BF16),
            pltpu.VMEM((chips, cols, tokens), BF16),
            pltpu.VMEM((bands, cols, tokens), F32),
            pltpu.VMEM((groups, cols, tokens), F32),
            pltpu.VMEM((2 * groups, tokens), F32),
            pltpu.VMEM((2 * groups + 8, tokens), F32),
            pltpu.VMEM((peers, 2 * groups, tokens), F32),
            pltpu.VMEM((peers, 2 * groups + 8, tokens), F32),
            pltpu.VMEM((peers, cols, tokens), BF16),
            pltpu.VMEM((cols, tokens), F32),
            pltpu.VMEM((bands, cols, tokens), BF16),
            pltpu.VMEM((sections, rows, cols), BF16),
            pltpu.VMEM((2, 2, 4, rows, cols), BF16),
            pltpu.VMEM((rows, cols), BF16),
            pltpu.VMEM((rows, cols), BF16),
            pltpu.VMEM((cols, tokens), F32),
            dma((2,)),
            dma((peers,)),
            dma((4,)),
            dma((chips,)),
            dma((peers,)),
            dma((chips,)),
            dma((chips,)),
            dma((chips,)),
            dma((chips,)),
            dma((chips,)),
            dma((peers,)),
            dma((peers,)),
            dma((peers,)),
            dma((peers,)),
            dma((chips,)),
            dma((peers,)),
            dma((chips,)),
            dma((2, 2, 4)),
            dma((2, 2, 4)),
            dma,
            dma,
        ],
        compiler_params=pltpu.CompilerParams(
            collective_id=0, has_side_effects=True, vmem_limit_bytes=60 * 1024 * 1024
        ),
    )(
        band_pick.T,
        band_count,
        plan,
        pixels.transpose(1, 0, 2),
        tok_gain,
        trunk_gain.reshape(-1, 128),
        query_cot.T,
        resid_cot.T,
        bands_weight.transpose(0, 2, 1),
        query_weight.T,
    )
    return (queries.T, grads.reshape(bands, rows // bands, cols))


def solution(mesh):
    placed = (
        P("mp", None, None),
        P(),
        P(),
        P(None, "mp"),
        P(None, None, "mp"),
        P(),
        P(),
        P(None, "mp"),
        P("section", "mp"),
        P("section", "mp"),
    )
    return jax.shard_map(
        body,
        mesh=mesh,
        in_specs=placed,
        out_specs=(P("section", "mp"), P(None, "section", "mp")),
        check_vma=False,
    )
```

time: 163 us -> 101 us (0.62)
  Pallas kernels: 136 us -> 95.7 us
  local copies, waits for them, and re-layouts: 26 us -> 3.17 us
    pallas_call x1, Pallas kernels: 136 us -> 95.7 us  [body(): pl.pallas_call(functools.partial(kernel, model_width), out_shape=(jax.Sha...]
    unnamed x7 -> x2, local copies, waits for them, and re-layouts: 22.5 us -> 3.17 us
    reshape x2 -> x0, local copies, waits for them, and re-layouts: 3.53 us -> none  [the longest x1 2.09 us: body(): pixels.reshape(tokens // TILE, TILE, bands, patch).transpose(0, 2, 1, 3)]
where the time goes in v2:
time: 101 us; the launch traced here: 99.5 us
  Pallas kernels  95.7 us (95%)
  local copies, waits for them, and re-layouts  3.17 us (3%)
    pallas_call x1, Pallas kernels, body(): pl.pallas_call(functools.partial(kernel, model_width), out_shape=(jax.Sha...  95.7 us
    unnamed x2, local copies, waits for them, and re-layouts  3.17 us

profile of v2, /device:TPU:1, one launch (start us, length us, event | category | flops | bytes accessed | tf_op | source)
XLA Modules:
  0.0 99.5 jit_solution(7217127996006075589)
XLA Ops:
  0.6 95.7 %shard_map.113 = (bf16[448,128]{1,0:T(8,128)(2,1)}, bf16[192,448]{1,0:T(8,128)(2,1)}) custom-call(s32[4,16]{1,0:T(4,128)} %bitcast.17, s32[16]{0:T(128)} %count_ref.1, s32[4]{0:T(128)} %plan_ref.1, bf16[12,128,256]{2,1,0:T(8,128)(2,1)} %bitcast.11, f32[16,448]{1,0:T(8,128)} %gain_ref.1, f32[56,128]{1,0:T(8,128)} %bitcast.16, bf16[448,128]{1,0:T(8,128)(2,1)} %bitcast.13, ...), custom_call_target="tpu_custom_call" | custom-call | tf_op jit(solution)/shard_map/pallas_call | solution.py:522
  96.4 1.6 %copy.14 = bf16[128,448]{0,1:T(8,128)(2,1)} copy(bf16[128,448]{0,1:T(8,128)(2,1)} %bitcast.15) | data formatting | bytes 229376
  97.9 1.6 %copy.15 = bf16[12,16,448]{2,1,0:T(8,128)(2,1)} copy(bf16[12,16,448]{2,1,0:T(8,128)(2,1)} %bitcast.12) | data formatting | bytes 344064

commit v3 on v2

v3 whole, which is shorter than its diff:
```python
import functools

import jax
import jax.numpy as jnp
from jax import lax
from jax.experimental import pallas as pl
from jax.experimental.pallas import tpu as pltpu
from jax.sharding import PartitionSpec as P

EPSILON = 1e-05
MESH = pl.DeviceIdType.MESH
F32 = jnp.float32
BF16 = jnp.bfloat16
NEAR = 8
TILE = 16
STEP = 112


def kernel(
    model_width,
    pick_ref,
    count_ref,
    plan_ref,
    pix_ref,
    gain_ref,
    tg_ref,
    qc_ref,
    rc_ref,
    w_hbm,
    wq_hbm,
    q_ref,
    bg_ref,
    live,
    member,
    w_ref,
    wq_ref,
    qc_rows,
    gain_wide,
    tg_wide,
    cand,
    xg,
    xt,
    stage,
    pre,
    crecv,
    p_ref,
    go,
    rows1,
    rows2,
    rows3,
    twin1,
    twin2,
    twin3,
    ps1,
    ps2,
    ps3,
    ag,
    tgng,
    gb,
    pb,
    cr,
    ybuf,
    yrecv,
    acc,
    local_sem,
    cand_send,
    cand_recv,
    x_send,
    x_recv,
    x_pass,
    pre_send,
    pre_recv,
    c_send,
    c_recv,
    p1_send,
    p1_recv,
    p2_send,
    p2_recv,
    p3_send,
    p3_recv,
    twin_send,
    twin_recv,
    ag_send,
    ag_recv,
    ag_pass,
    cr_send,
    cr_recv,
    y_send,
    y_recv,
):
    slots, groups = pick_ref.shape
    bands, tokens, patch = xg.shape
    cols = qc_ref.shape[0]
    peers = ag.shape[0]
    chips = peers // 2
    half_bands = bands // 2
    me = lax.axis_index("mp")
    chip = me // 2
    core = lax.rem(me, 2)
    twin = me + 1 - 2 * core
    section = lax.axis_index("section")
    half = section // NEAR
    ring = lax.rem(section, NEAR)
    low = lax.rem(section, 4)
    block = section // 4

    copy_wq = pltpu.make_async_copy(wq_hbm, wq_ref, local_sem.at[0])
    copy_w = pltpu.make_async_copy(w_hbm, w_ref, local_sem.at[1])
    copy_wq.start()
    copy_w.start()

    def peer(i):
        return lax.rem(me + i, peers)

    def near(i):
        return lax.rem(chip + i, chips)

    def at_ring(step):
        return half * NEAR + lax.rem(ring + step + NEAR, NEAR)

    down, up = at_ring(-1), at_ring(1)
    across = (1 - half) * NEAR + ring

    barrier = pltpu.get_barrier_semaphore()

    @pl.loop(1, peers)
    def _(i):
        pl.semaphore_signal(barrier, inc=1, device_id={"mp": peer(i)}, device_id_type=MESH)

    for other in (down, up, across):
        pl.semaphore_signal(barrier, inc=1, device_id={"section": other}, device_id_type=MESH)

    def remote(src, dst, send, recv, axis, to):
        return pltpu.make_async_remote_copy(
            src_ref=src,
            dst_ref=dst,
            send_sem=send,
            recv_sem=recv,
            device_id={axis: to},
            device_id_type=MESH,
        )

    @pl.loop(0, groups)
    def _(g):
        used = count_ref[g]
        for k in range(slots):
            live[g, k] = jnp.where(k < used, 1.0, 0.0).astype(F32)
        for b in range(bands):
            hit = jnp.float32(0.0)
            for k in range(slots):
                same = jnp.logical_and(pick_ref[k, g] == b, k < used)
                hit = hit + jnp.where(same, 1.0, 0.0).astype(F32)
            member[g, b] = hit

    qc_rows[...] = qc_ref[...].T

    copy_wq.wait()

    @pl.loop(0, chips)
    def _(k):
        at = pl.ds(pl.multiple_of(k * 2 * cols, 128), 2 * cols)
        tiles = jnp.dot(qc_rows[...], wq_ref[:, at], preferred_element_type=F32).T
        stage[2 * k] = tiles[:cols].astype(BF16)
        stage[2 * k + 1] = tiles[cols:].astype(BF16)

    pl.semaphore_wait(barrier, peers - 1 + 3)

    def piece(ref, j):
        start = pl.multiple_of((j // 2) * TILE, TILE)
        return ref.at[pl.ds(lax.rem(j, 2) * half_bands, half_bands), pl.ds(start, TILE), :]

    def cand_copy(i):
        to = peer(i)
        slot = me // 4
        return remote(
            piece(pix_ref, to), cand.at[slot], cand_send.at[i], cand_recv.at[slot], "mp", to
        )

    owner = lax.rem(me, 4) == low

    @pl.when(owner)
    def _():
        pltpu.make_async_copy(piece(pix_ref, me), cand.at[me // 4], cand_recv.at[me // 4]).start()

        @pl.loop(1, peers)
        def _(i):
            cand_copy(i).start()

    def pre_copy(k):
        return remote(
            stage.at[2 * k + 1 - core], pre.at[k], pre_send.at[k], pre_recv.at[k], "mp", twin
        )

    @pl.loop(1, chips)
    def _(i):
        pre_copy(near(i)).start()

    pre_copy(chip).start()

    gain_cols = gain_ref[...].T
    for g in range(groups):
        gain_wide[g] = jnp.broadcast_to(gain_cols[:, g : g + 1], (cols, tokens))

    def cross_copy(i):
        k = near(i)
        return remote(
            stage.at[2 * k + core], crecv.at[chip], c_send.at[i], c_recv.at[chip], "mp", 2 * k + core
        )

    def cross_out(i):
        k = near(i)
        pltpu.make_async_copy(pre.at[k], pre.at[k], pre_recv.at[k]).wait()
        stage[2 * k + core] = (stage[2 * k + core].astype(F32) + pre[k].astype(F32)).astype(BF16)
        cross_copy(i).start()

    early = 3

    @pl.loop(1, early)
    def _(i):
        cross_out(i)

    for c in range(4):
        pltpu.make_async_copy(cand.at[c], cand.at[c], cand_recv.at[c]).wait()

    def spread(view, send, recv):
        own = view(me)
        remote(own, own, send.at[0], recv.at[me], "mp", twin).start()

        @pl.loop(1, chips)
        def _(i):
            remote(own, own, send.at[i], recv.at[me], "mp", 2 * near(i) + core).start()

    def spread_wait(view, recv, hand):
        @pl.loop(1, chips)
        def _(i):
            src = 2 * near(i) + core
            block_of = view(src)
            pltpu.make_async_copy(block_of, block_of, recv.at[src]).wait()
            remote(block_of, block_of, hand.at[i], recv.at[src], "mp", twin).start()

        @pl.loop(0, chips)
        def _(i):
            src = 2 * near(i) + 1 - core
            block_of = view(src)
            pltpu.make_async_copy(block_of, block_of, recv.at[src]).wait()

    def spread_end(view, send, hand):
        own = view(me)

        @pl.loop(0, chips)
        def _(i):
            pltpu.make_async_copy(own, own, send.at[i]).wait()

        @pl.loop(1, chips)
        def _(i):
            pltpu.make_async_copy(own, own, hand.at[i]).wait()

    def x_view(j):
        return piece(xg, j)

    mine = pl.ds(pl.multiple_of(chip * TILE, TILE), TILE)
    xg[pl.ds(core * half_bands, half_bands), mine, :] = cand[plan_ref[block]]
    spread(x_view, x_send, x_recv)

    @pl.loop(early, chips)
    def _(i):
        cross_out(i)

    pltpu.make_async_copy(pre.at[chip], pre.at[chip], pre_recv.at[chip]).wait()
    crecv[chip] = (stage[2 * chip + core].astype(F32) + pre[chip].astype(F32)).astype(BF16)

    tg_cols = tg_ref[...].T
    for k in range(tg_ref.shape[0]):
        tg_wide[128 * k : 128 * (k + 1), :] = jnp.broadcast_to(tg_cols[:, k : k + 1], (128, tokens))

    copy_w.wait()
    spread_wait(x_view, x_recv, x_pass)

    @pl.loop(0, bands)
    def _(b):
        p_ref[b] = lax.dot_general(
            w_ref[b], xg[b], (((1,), (1,)), ((), ())), preferred_element_type=F32
        )

    def fold(value):
        return jnp.sum(value.reshape(-1, 8, tokens), axis=0)

    def line(value):
        return jnp.sum(value, axis=0, keepdims=True)

    steps = range(0, cols, STEP)

    @pl.loop(0, groups)
    def _(g):
        square = jnp.zeros((8, tokens), F32)
        for d in steps:
            at = slice(d, d + STEP)
            out = live[g, 0] * p_ref[pick_ref[0, g], at, :]
            for k in range(1, slots):
                out = out + live[g, k] * p_ref[pick_ref[k, g], at, :]
            go[g, at, :] = out
            square = square + fold(out * out)
        rows1[pl.ds(g, 1), :] = line(square)

    def twin_copy(n, rows, there):
        return remote(rows, there, twin_send.at[n], twin_recv.at[n], "mp", twin)

    def chip_copy(buf, send, recv, i):
        return remote(
            buf.at[chip], buf.at[chip], send.at[i], recv.at[chip], "mp", 2 * near(i) + core
        )

    def to_chips(n, rows, there, buf, send, recv):
        twin_copy(n, rows, there).wait_recv()
        buf[chip] = rows[...] + there[...]

        @pl.loop(1, chips)
        def _(i):
            chip_copy(buf, send, recv, i).start()

    def total(buf, recv):
        @pl.loop(1, chips)
        def _(i):
            k = near(i)
            pltpu.make_async_copy(buf.at[k], buf.at[k], recv.at[k]).wait()

        value = buf[0]
        for i in range(1, chips):
            value = value + buf[i]
        return value

    def sum_end(n, rows, there, buf, send, recv):
        twin_copy(n, rows, there).wait_send()

        @pl.loop(1, chips)
        def _(i):
            chip_copy(buf, send, recv, i).wait_send()

    sum1 = (0, rows1, twin1, ps1, p1_send, p1_recv)
    sum2 = (1, rows2, twin2, ps2, p2_send, p2_recv)
    sum3 = (2, rows3, twin3, ps3, p3_send, p3_recv)

    twin_copy(0, rows1, twin1).start()

    @pl.loop(0, bands // 2)
    def _(b):
        xt[b] = xg[b].T

    to_chips(*sum1)

    @pl.loop(bands // 2, bands)
    def _(b):
        xt[b] = xg[b].T

    @pl.loop(1, chips)
    def _(i):
        k = near(i)
        pltpu.make_async_copy(crecv.at[k], crecv.at[k], c_recv.at[k]).wait()

    own_rows = pl.multiple_of(me * cols, 64)
    for d in steps:
        at = slice(d, d + STEP)
        grad = crecv[0, at, :].astype(F32)
        for i in range(1, chips):
            grad = grad + crecv[i, at, :].astype(F32)
        tgng[at, :] = grad * tg_wide[pl.ds(own_rows + d, STEP), :]

    @pl.loop(0, groups)
    def _(g):
        with_resid = jnp.zeros((8, tokens), F32)
        with_grad = jnp.zeros((8, tokens), F32)
        for d in steps:
            at = slice(d, d + STEP)
            unit = go[g, at, :] * gain_wide[g, at, :]
            with_resid = with_resid + fold(unit * rc_ref[at, :].astype(F32))
            with_grad = with_grad + fold(unit * tgng[at, :])
        rows2[pl.ds(g, 1), :] = line(with_resid)
        rows2[pl.ds(groups + g, 1), :] = line(with_grad)

    twin_copy(1, rows2, twin2).start()
    scale = lax.rsqrt(total(ps1, p1_recv) / model_width + EPSILON)

    trunk_square = jnp.zeros((8, tokens), F32)
    trunk_grad = jnp.zeros((8, tokens), F32)
    for d in range(0, cols, 32):
        at = slice(d, d + 32)
        value = jnp.zeros((32, tokens), F32)
        for g in range(groups):
            value = value + go[g, at, :] * scale[g : g + 1, :] * gain_wide[g, at, :]
        low_value = value.astype(BF16)
        ag[me, at, :] = low_value
        trunk = low_value.astype(F32)
        trunk_square = trunk_square + fold(trunk * trunk)
        trunk_grad = trunk_grad + fold(trunk * tgng[at, :])
    rows3[groups : groups + 1, :] = line(trunk_square)
    rows3[groups + 1 : groups + 2, :] = line(trunk_grad)
    rows3[groups + 2 :, :] = jnp.zeros((6, tokens), F32)

    @pl.loop(0, groups)
    def _(g):
        with_trunk = jnp.zeros((8, tokens), F32)
        for d in steps:
            at = slice(d, d + STEP)
            unit = go[g, at, :] * gain_wide[g, at, :]
            with_trunk = with_trunk + fold(unit * ag[me, at, :].astype(F32))
        rows3[pl.ds(g, 1), :] = line(with_trunk)

    twin_copy(2, rows3, twin3).start()
    to_chips(*sum2)
    to_chips(*sum3)

    def ag_view(j):
        return ag.at[j]

    spread(ag_view, ag_send, ag_recv)
    second = total(ps2, p2_recv)
    third = total(ps3, p3_recv)
    row_scale = lax.rsqrt(third[groups : groups + 1] / model_width + EPSILON)
    row_stat = third[groups + 1 : groups + 2] / model_width
    cube_stat = row_scale * row_scale * row_scale * row_stat
    group_stat = (
        second[:groups] + row_scale * second[groups:] - cube_stat * third[:groups]
    ) / model_width
    cube_group = scale * scale * scale * group_stat

    for d in range(0, cols, 32):
        at = slice(d, d + 32)
        grad = (
            rc_ref[at, :].astype(F32)
            + row_scale * tgng[at, :]
            - cube_stat * ag[me, at, :].astype(F32)
        )
        grad = grad.astype(BF16).astype(F32)
        for g in range(groups):
            go[g, at, :] = (
                scale[g : g + 1, :] * (grad * gain_wide[g, at, :])
                - go[g, at, :] * cube_group[g : g + 1, :]
            )

    def unit(way, h, t):
        offset = (4 - t) if way else (t - 4)
        side = half if h else 1 - half
        return side * NEAR + lax.rem(ring + offset + NEAR, NEAR)

    def link(way, h, j, t):
        return remote(
            pb.at[unit(way, h, t), j],
            cr.at[way, h, j, t],
            cr_send.at[way, h, j, t],
            cr_recv.at[way, h, j, t],
            "section",
            up if way else down,
        )

    def first_step(way, h):
        return 0 if way == h else 1

    def begin(h, j):
        for way in range(2):
            link(way, h, j, first_step(way, h)).start()

    def advance(h, j, n):
        for way in range(2):
            t = first_step(way, h) + n
            if t < 4:
                link(way, h, j, t - 1).wait_recv()
                at = unit(way, h, t)
                pb[at, j] = (pb[at, j].astype(F32) + cr[way, h, j, t - 1].astype(F32)).astype(BF16)
                link(way, h, j, t).start()

    def gathered(h, j):
        side = half if h else 1 - half
        link(0, h, j, 3).wait_recv()
        link(1, h, j, 3).wait_recv()
        return (
            pb[side * NEAR + ring, j].astype(F32)
            + cr[0, h, j, 3].astype(F32)
            + cr[1, h, j, 3].astype(F32)
        )

    def over(j):
        return remote(ybuf.at[j], yrecv.at[j], y_send.at[j], y_recv.at[j], "section", across)

    for j in range(2):

        @pl.loop(0, cols // 32)
        def _(r):
            at = pl.ds(pl.multiple_of(r * 32, 32), 32)
            found = [jnp.zeros((32, tokens), F32) for _ in range(half_bands)]
            for g in range(groups):
                value = go[g, at, :]
                found = [
                    found[d] + member[g, half_bands * j + d] * value for d in range(half_bands)
                ]
            for d in range(half_bands):
                gb[d, at, :] = found[d].astype(BF16)

        @pl.loop(0, half_bands // 2)
        def _(n):
            rests = []
            for e in range(2):
                value = lax.dot_general(
                    xt[half_bands * j + 2 * n + e],
                    gb[2 * n + e],
                    (((1,), (1,)), ((), ())),
                    preferred_element_type=F32,
                )
                value = value.reshape(pb.shape[0], TILE, cols)
                for c in range(3):
                    rows = pl.ds(pl.multiple_of((6 * n + 3 * e + c) * TILE, TILE), TILE)
                    pb[:, j, rows, :] = value[:, :, 128 * c : 128 * (c + 1)].astype(BF16)
                rests.append(value[:, :, 384:])
            rows = pl.ds(pl.multiple_of((3 * half_bands + n) * TILE, TILE), TILE)
            pb[:, j, rows, :] = jnp.concatenate(rests, axis=2).astype(BF16)

        begin(0, j)

    advance(0, 0, 1)
    advance(0, 1, 1)
    begin(1, 0)
    advance(0, 0, 2)
    advance(0, 1, 2)
    begin(1, 1)
    spread_wait(ag_view, ag_recv, ag_pass)
    advance(0, 0, 3)
    advance(0, 1, 3)
    advance(1, 0, 1)
    advance(1, 1, 1)
    for j in range(2):
        ybuf[j] = gathered(0, j).astype(BF16)
        over(j).start()
    for n in (2, 3):
        for j in range(2):
            advance(1, j, n)

    acc[...] = jnp.zeros_like(acc)

    @pl.loop(0, chips)
    def _(k):
        rows = pl.ds(pl.multiple_of(k * 2 * cols, 128), 2 * cols)
        trunk = ag[pl.ds(2 * k, 2)].reshape(2 * cols, tokens).astype(F32)
        normed = (trunk * row_scale * tg_wide[rows, :]).astype(BF16)
        acc[...] += jnp.dot(wq_ref[:, rows], normed, preferred_element_type=F32)

    q_ref[...] = acc[...].astype(BF16)
    for j in range(2):
        own_sum = gathered(1, j)
        over(j).wait_recv()
        bg_ref[j] = (own_sum + yrecv[j].astype(F32)).astype(BF16)

    for j in range(2):
        over(j).wait_send()
        for h in range(2):
            for way in range(2):
                for t in range(first_step(way, h), 4):
                    link(way, h, j, t).wait_send()

    @pl.when(owner)
    def _():
        @pl.loop(1, peers)
        def _(i):
            cand_copy(i).wait_send()

    spread_end(x_view, x_send, x_pass)
    spread_end(ag_view, ag_send, ag_pass)

    @pl.loop(0, chips)
    def _(k):
        pre_copy(k).wait_send()

    @pl.loop(1, chips)
    def _(i):
        cross_copy(i).wait_send()

    for each in (sum1, sum2, sum3):
        sum_end(*each)


def place(bands, q_ref, bg_ref, q_out, bg_out):
    half_bands = bands // 2
    q_out[...] = q_ref[...]
    for b in range(bands):
        j, d = b // half_bands, b % half_bands
        for c in range(3):
            rows = (3 * d + c) * TILE
            bg_out[b, :, 128 * c : 128 * (c + 1)] = bg_ref[j, rows : rows + TILE, :]
        rows = (3 * half_bands + d // 2) * TILE
        side = 64 * (d % 2)
        bg_out[b, :, 384:] = bg_ref[j, rows : rows + TILE, side : side + 64]


def body(
    pixels,
    band_pick,
    band_count,
    tok_gain,
    bands_weight,
    plan,
    trunk_gain,
    query_weight,
    query_cot,
    resid_cot,
):
    peers = lax.axis_size("mp")
    chips = peers // 2
    sections = lax.axis_size("section")
    groups = band_pick.shape[0]
    tokens, bands, patch = pixels.shape
    cols = bands_weight.shape[2]
    model_width = cols * peers
    rows = bands * patch // sections
    packed = (2, rows * cols // 256, 128)
    vmem = pl.BlockSpec(memory_space=pltpu.VMEM)
    smem = pl.BlockSpec(memory_space=pltpu.SMEM)
    hbm = pl.BlockSpec(memory_space=pl.ANY)
    dma = pltpu.SemaphoreType.DMA
    queries, grads = pl.pallas_call(
        functools.partial(kernel, model_width),
        out_shape=(
            jax.ShapeDtypeStruct((cols, tokens), BF16),
            jax.ShapeDtypeStruct(packed, BF16),
        ),
        in_specs=[smem] * 3 + [hbm] + [vmem] * 4 + [hbm] * 2,
        out_specs=(vmem, vmem),
        scratch_shapes=[
            pltpu.SMEM((groups, band_pick.shape[1]), F32),
            pltpu.SMEM((groups, bands), F32),
            pltpu.VMEM((bands, cols, patch), BF16),
            pltpu.VMEM((cols, model_width), BF16),
            pltpu.VMEM((tokens, cols), BF16),
            pltpu.VMEM((groups, cols, tokens), F32),
            pltpu.VMEM((model_width, tokens), F32),
            pltpu.VMEM((4, bands // 2, TILE, patch), BF16),
            pltpu.VMEM((bands, tokens, patch), BF16),
            pltpu.VMEM((bands, patch, tokens), BF16),
            pltpu.VMEM((peers, cols, tokens), BF16),
            pltpu.VMEM((chips, cols, tokens), BF16),
            pltpu.VMEM((chips, cols, tokens), BF16),
            pltpu.VMEM((bands, cols, tokens), F32),
            pltpu.VMEM((groups, cols, tokens), F32),
            pltpu.VMEM((groups, tokens), F32),
            pltpu.VMEM((2 * groups, tokens), F32),
            pltpu.VMEM((groups + 8, tokens), F32),
            pltpu.VMEM((groups, tokens), F32),
            pltpu.VMEM((2 * groups, tokens), F32),
            pltpu.VMEM((groups + 8, tokens), F32),
            pltpu.VMEM((chips, groups, tokens), F32),
            pltpu.VMEM((chips, 2 * groups, tokens), F32),
            pltpu.VMEM((chips, groups + 8, tokens), F32),
            pltpu.VMEM((peers, cols, tokens), BF16),
            pltpu.VMEM((cols, tokens), F32),
            pltpu.VMEM((bands // 2, cols, tokens), BF16),
            pltpu.VMEM((sections,) + packed, BF16),
            pltpu.VMEM((2, 2, 2, 4) + packed[1:], BF16),
            pltpu.VMEM(packed, BF16),
            pltpu.VMEM(packed, BF16),
            pltpu.VMEM((cols, tokens), F32),
            dma((2,)),
            dma((peers,)),
            dma((4,)),
            dma((chips,)),
            dma((peers,)),
            dma((chips,)),
            dma((chips,)),
            dma((chips,)),
            dma((chips,)),
            dma((chips,)),
            dma((chips,)),
            dma((chips,)),
            dma((chips,)),
            dma((chips,)),
            dma((chips,)),
            dma((chips,)),
            dma((3,)),
            dma((3,)),
            dma((chips,)),
            dma((peers,)),
            dma((chips,)),
            dma((2, 2, 2, 4)),
            dma((2, 2, 2, 4)),
            dma((2,)),
            dma((2,)),
        ],
        compiler_params=pltpu.CompilerParams(
            collective_id=0, has_side_effects=True, vmem_limit_bytes=60 * 1024 * 1024
        ),
    )(
        band_pick.T,
        band_count,
        plan,
        pixels.transpose(1, 0, 2),
        tok_gain,
        trunk_gain.reshape(-1, 128),
        query_cot.T,
        resid_cot.T,
        bands_weight.transpose(0, 2, 1),
        query_weight.T,
    )
    queries, grads = pl.pallas_call(
        functools.partial(place, bands),
        out_shape=(
            jax.ShapeDtypeStruct((cols, tokens), BF16),
            jax.ShapeDtypeStruct((bands, rows // bands, cols), BF16),
        ),
        in_specs=[vmem] * 2,
        out_specs=(vmem, vmem),
    )(queries, grads)
    return (queries.T, grads)


def solution(mesh):
    placed = (
        P("mp", None, None),
        P(),
        P(),
        P(None, "mp"),
        P(None, None, "mp"),
        P(),
        P(),
        P(None, "mp"),
        P("section", "mp"),
        P("section", "mp"),
    )
    return jax.shard_map(
        body,
        mesh=mesh,
        in_specs=placed,
        out_specs=(P("section", "mp"), P(None, "section", "mp")),
        check_vma=False,
    )
```

time: 101 us -> 95.1 us (0.942)
  the two profiles are of different devices: /device:TPU:1 before, /device:TPU:6 now
where the time goes in v3:
time: 95.1 us; the launch traced here: 95 us
  Pallas kernels  94.3 us (99%)
    pallas_call x1, Pallas kernels, body(): pl.pallas_call(functools.partial(kernel, model_width), out_shape=(jax.Sha...  92.6 us

profile of v3, /device:TPU:6, one launch (start us, length us, event | category | flops | bytes accessed | tf_op | source)
XLA Modules:
  0.0 95.0 jit_solution(4209138724041645737)
XLA Ops:
  0.6 92.6 %shard_map.113 = (bf16[448,128]{1,0:T(8,128)(2,1)}, bf16[2,336,128]{2,1,0:T(8,128)(2,1)}) custom-call(s32[4,16]{1,0:T(4,128)} %bitcast.14, s32[16]{0:T(128)} %count_ref.1, s32[4]{0:T(128)} %plan_ref.1, bf16[12,128,256]{2,1,0:T(8,128)(2,1)} %bitcast.10, f32[16,448]{1,0:T(8,128)} %gain_ref.1, f32[56,128]{1,0:T(8,128)} %bitcast.13, bf16[448,128]{1,0:T(8,128)(2,1)} %bitcast.11, ...), custom_call_target="tpu_custom_call" | custom-call | tf_op jit(solution)/shard_map/pallas_call | solution.py:617
  93.2 1.7 %shard_map.114 = (bf16[448,128]{1,0:T(8,128)(2,1)}, bf16[12,16,448]{2,1,0:T(8,128)(2,1)}) custom-call(bf16[448,128]{1,0:T(8,128)(2,1)} %get-tuple-element.6.q_ref, bf16[2,336,128]{2,1,0:T(8,128)(2,1)} %get-tuple-element.7.bg_ref), custom_call_target="tpu_custom_call" | custom-call | tf_op jit(solution)/shard_map/pallas_call | solution.py:699
